TPU v7x, 256 devices: a whole 4x4x8 slice. The times are simulated.
256 devices in a mesh: lev: 8 (over z_hi, y), tile: 32 (over z_lo, x, core).
Axes of the slice: x: 4, y: 4, z: 8 (z_hi: 2, z_lo: 4; z = z_hi * 4 + z_lo), core: 2. Of those that a mesh axis runs over, the one named last changes fastest.
Arguments:
- prognostic: float32 [4, 128, 262144], P(None, 'lev', 'tile'), may hold values from -6 to 6
- neighbours: int32 [4, 262144], P(None, 'tile'), may hold values from 0 to 8447, as said below
- metric: float32 [2, 4, 262144], P(None, None, 'tile'), may hold values from -0.9 to 0.9
- inverses: float32 [32, 128, 128], P('tile')
Outputs:
- advanced: float32 [4, 128, 262144], P(None, 'lev', 'tile')
Inputs may be any that keep to these rules, and one draw needn't show every extreme that they name: `neighbours`: entry [k, c] indexes the cells of c's tile extended by 128 cells on each side: 0 to 127 are the last 128 cells of the previous tile, then the tile's own 8192 cells in order, then the first 128 cells of the next tile, the tiles forming a closed cycle; each entry lies within 128 of 128 + (c mod 8192).
All inputs are finite; a program needn't handle non-finite values.
Results may differ from a plain program's by a relative error of at most 0.0001.
Values sent between devices are 32-bit elements; how exact they have to be, the bound alone decides.
A program may use at most 64 MiB of HBM per device.

v0:
```python
import functools

import jax
import jax.numpy as jnp
from jax import lax
from jax.experimental import pallas as pl
from jax.experimental.pallas import tpu as pltpu
from jax.sharding import PartitionSpec as P

SUBSTEPS = 3
NB = 4
HALO = 128
NY = 4
BLOCK = 256
LAG = 4
F32, BF16 = jnp.float32, jnp.bfloat16
C = 0.4 * 0.5


def split(x):
    high = x.astype(BF16)
    return high, (x - high.astype(F32)).astype(BF16)


def dot(a, b):
    return jnp.dot(a, b, preferred_element_type=F32)


def kernel(prog, nbrs, metr, inv, out, X, PP, RS, RR, PB, PQ, M, NBV, MTV, IH, IL,
           lsem, yin_s, yin_r, yin_l, out_s, out_r, out_l, z_s, z_r, b_s, b_r, h_s, h_r):
    lev, tile = lax.axis_index("lev"), lax.axis_index("tile")
    zh, y = lev // NY, lev % NY
    tiles = lax.axis_size("tile")
    half = X.shape[2]
    rows16 = half // NY
    slab = PP.shape[2]
    blocks = slab // BLOCK
    total = SUBSTEPS * blocks

    def at(yy, tt):
        return {"lev": zh * NY + yy, "tile": tt}

    peers = [at((y + d) % NY, tile) for d in range(NY)]
    partner = {"lev": (1 - zh) * NY + y, "tile": tile}
    right = at((y + 1) % NY, (tile + jnp.where(y == NY - 1, 1, 0)) % tiles)
    left = at((y + NY - 1) % NY, (tile + jnp.where(y == 0, tiles - 1, 0)) % tiles)

    def remote(src, dst, ssem, rsem, dev):
        return pltpu.make_async_remote_copy(src, dst, ssem, rsem, device_id=dev, device_id_type=pl.DeviceIdType.MESH)

    def order(i):
        return jnp.where(i % 2 == 0, i // 2, blocks - 1 - i // 2)

    def cells(c):
        return pl.ds(pl.multiple_of(HALO + c * BLOCK, 128), BLOCK)

    def lanes(c):
        return pl.ds(pl.multiple_of(c * BLOCK, 128), BLOCK)

    def y_in(c, d):
        yy = (y + d) % NY
        src = prog.at[:, :, pl.ds(pl.multiple_of(yy * slab + c * BLOCK, 128), BLOCK)]
        dst = X.at[0, :, pl.ds(pl.multiple_of(y * rows16, 8), rows16), cells(c)]
        if d == 0:
            return pltpu.make_async_copy(src, dst, yin_l.at[c])
        return remote(src, dst, yin_s.at[c, d - 1], yin_r.at[c, d - 1], peers[d])

    def y_in_start(c):
        for d in range(NY):
            y_in(c, d).start()

    def y_in_wait(c):
        y_in(c, 0).wait()
        for d in range(1, NY):
            y_in(c, d).wait_recv()

    def y_out(f, c, d):
        yy = (y + d) % NY
        src = X.at[SUBSTEPS, pl.ds(2 * f, 2), pl.ds(pl.multiple_of(yy * rows16, 8), rows16), cells(c)]
        dst = out.at[pl.ds(2 * f, 2), :, pl.ds(pl.multiple_of(y * slab + c * BLOCK, 128), BLOCK)]
        if d == 0:
            return pltpu.make_async_copy(src, dst, out_l.at[f, c])
        return remote(src, dst, out_s.at[f, c, d - 1], out_r.at[f, c, d - 1], peers[d])

    def z_copies(s, c):
        return (
            remote(RS.at[s, :, lanes(c)], RR.at[s, :, lanes(c)], z_s.at[s, c], z_r.at[s, c], partner),
            remote(PB.at[s, c], PQ.at[s, c], b_s.at[s, c], b_r.at[s, c], partner),
        )

    def halo(s, side):
        if side == 0:
            src, dst, dev = pl.ds(HALO, HALO), pl.ds(HALO + slab, HALO), left
        else:
            src, dst, dev = pl.ds(slab, HALO), pl.ds(0, HALO), right
        return remote(X.at[s, pl.ds(0, 3), :, src], X.at[s, pl.ds(0, 3), :, dst], h_s.at[s, side], h_r.at[s, side], dev)

    barrier = pltpu.get_barrier_semaphore()
    others = peers[1:] + [partner, left, right]
    for dev in others:
        pl.semaphore_signal(barrier, 1, device_id=dev, device_id_type=pl.DeviceIdType.MESH)
    local = (
        pltpu.make_async_copy(nbrs.at[:, pl.ds(pl.multiple_of(y * slab, 128), slab)], NBV, lsem.at[0]),
        pltpu.make_async_copy(metr.at[:, :, pl.ds(pl.multiple_of(y * slab, 128), slab)], MTV, lsem.at[1]),
    )
    for copy in local:
        copy.start()
    pl.semaphore_wait(barrier, len(others))
    for i in range(3):
        y_in_start(order(i))
    for copy in local:
        copy.wait()

    full = inv[0]
    swapped = jnp.where(zh == 0, full, pltpu.roll(full, half, 1))
    mine = jnp.concatenate([
        jnp.where(zh == 0, swapped[:half], swapped[half:]),
        jnp.where(zh == 0, swapped[half:half + 8], swapped[half - 8:half]),
    ])
    IH[...], IL[...] = split(mine)

    level = lax.broadcasted_iota(jnp.int32, (half, BLOCK), 0)
    first, last = level == 0, level == half - 1

    def build(c):
        def rows(j, carry):
            r0 = pl.multiple_of(j * 64, 64)
            slot = lax.broadcasted_iota(jnp.int32, (64, BLOCK), 0) + r0
            cell = lax.broadcasted_iota(jnp.int32, (64, BLOCK), 1)
            here = slot == cell + HALO
            m0 = jnp.zeros((64, BLOCK), F32)
            m1 = jnp.zeros((64, BLOCK), F32)
            for k in range(NB):
                w0, w1 = MTV[0, pl.ds(k, 1), lanes(c)], MTV[1, pl.ds(k, 1), lanes(c)]
                hit = slot == NBV[pl.ds(k, 1), lanes(c)] - (y * slab + c * BLOCK)
                m0 = m0 + (jnp.where(hit, w0, 0.0) - jnp.where(here, w0, 0.0))
                m1 = m1 + (jnp.where(hit, w1, 0.0) - jnp.where(here, w1, 0.0))
            M[c, 0, pl.ds(r0, 64), :], M[c, 1, pl.ds(r0, 64), :] = split(m0)
            M[c, 2, pl.ds(r0, 64), :], M[c, 3, pl.ds(r0, 64), :] = split(m1)
            return carry

        lax.fori_loop(0, (BLOCK + 2 * HALO) // 64, rows, 0)

    def horizontal(s, c):
        window = pl.ds(pl.multiple_of(c * BLOCK, 128), BLOCK + 2 * HALO)
        uh, ul = split(X[s, 0, :, window])
        vh, vl = split(X[s, 1, :, window])
        ph, pl_ = split(X[s, 2, :, window])
        a0 = dot(jnp.concatenate([ph, uh, pl_, ul]), M[c, 0])
        b0 = dot(jnp.concatenate([ph, uh]), M[c, 1])
        a1 = dot(jnp.concatenate([ph, vh, pl_, vl]), M[c, 2])
        b1 = dot(jnp.concatenate([ph, vh]), M[c, 3])
        g0 = a0[: 2 * half] + a0[2 * half :] + b0
        g1 = a1[: 2 * half] + a1[2 * half :] + b1
        X[s + 1, 0, :, cells(c)] = X[s, 0, :, cells(c)] - g0[:half]
        X[s + 1, 1, :, cells(c)] = X[s, 1, :, cells(c)] - g1[:half]
        p = X[s, 2, :, cells(c)] - (g0[half:] + g1[half:])
        PP[s, :, lanes(c)] = p
        up = jnp.where(last, 0.0, pltpu.roll(p, half - 1, 0))
        down = jnp.where(first, 0.0, pltpu.roll(p, 1, 0))
        RS[s, :, lanes(c)] = X[s, 3, :, cells(c)] - C * (up - down)
        PB[s, c] = jnp.where(zh == 0, p[half - 1 :], p[:1])

    def vertical(s, c):
        top = jnp.where(zh == 0, 1.0, 0.0)
        own_b, other_b = PB[s, c], PQ[s, c]
        fix_own = jnp.where(last, -C * top, 0.0) + jnp.where(first, C * (1.0 - top), 0.0)
        fix_other = jnp.where(first, C * top, 0.0) + jnp.where(last, -C * (1.0 - top), 0.0)
        own = RS[s, :, lanes(c)] + fix_own * other_b
        other = RR[s, :, lanes(c)] + fix_other * own_b
        rh, rl = split(jnp.concatenate([own, other]))
        ih, il = IH[...], IL[...]
        w = dot(ih, rh) + (dot(ih, rl) + dot(il, rh))
        edge = jnp.where(zh == 0, w[half : half + 1], w[half + 7 : half + 8])
        w = w[:half]
        up = jnp.where(last, edge * top, pltpu.roll(w, half - 1, 0))
        down = jnp.where(first, edge * (1.0 - top), pltpu.roll(w, 1, 0))
        X[s + 1, 2, :, cells(c)] = PP[s, :, lanes(c)] - C * (up - down)
        X[s + 1, 3, :, cells(c)] = w

    def finish(t):
        s, c = t // blocks, order(t % blocks)
        for copy in z_copies(s, c):
            copy.wait_recv()
        vertical(s, c)

        @pl.when((s < SUBSTEPS - 1) & (c == 0))
        def _():
            halo(s + 1, 0).start()

        @pl.when((s < SUBSTEPS - 1) & (c == blocks - 1))
        def _():
            halo(s + 1, 1).start()

        @pl.when(s == SUBSTEPS - 1)
        def _():
            for d in range(NY):
                y_out(1, c, d).start()

    def begin(t):
        s, i = t // blocks, t % blocks
        c = order(i)

        @pl.when(s == 0)
        def _():
            @pl.when(i + 3 < blocks)
            def _():
                y_in_start(order(i + 3))

            build(c)

            @pl.when(i == 0)
            def _():
                y_in_wait(0)
                halo(0, 0).start()
                y_in_wait(blocks - 1)
                halo(0, 1).start()

            @pl.when(i + 2 < blocks)
            def _():
                y_in_wait(order(i + 2))

        @pl.when(i == 0)
        def _():
            halo(s, 1).wait_recv()

        @pl.when(i == 1)
        def _():
            halo(s, 0).wait_recv()

        horizontal(s, c)
        for copy in z_copies(s, c):
            copy.start()

        @pl.when(s == SUBSTEPS - 1)
        def _():
            for d in range(NY):
                y_out(0, c, d).start()

    def step(t, carry):
        @pl.when(t >= LAG)
        def _():
            finish(t - LAG)

        @pl.when(t < total)
        def _():
            begin(t)

        return carry

    lax.fori_loop(0, total + LAG, step, 0)

    def drain(c, carry):
        for d in range(1, NY):
            y_in(c, d).wait_send()
        for f in range(2):
            y_out(f, c, 0).wait()
            for d in range(1, NY):
                y_out(f, c, d).wait()
        for s in range(SUBSTEPS):
            for copy in z_copies(s, c):
                copy.wait_send()
        return carry

    lax.fori_loop(0, blocks, drain, 0)
    for s in range(SUBSTEPS):
        for side in range(2):
            halo(s, side).wait_send()


def per_device(prognostic, neighbours, metric, inverses):
    fields, rows16, cell_count = prognostic.shape
    half, slab = rows16 * NY, cell_count // NY
    blocks = slab // BLOCK
    dma = pltpu.SemaphoreType.DMA
    anywhere = pl.BlockSpec(memory_space=pl.ANY)
    return pl.pallas_call(
        kernel,
        name="acoustic",
        out_shape=jax.ShapeDtypeStruct(prognostic.shape, F32),
        in_specs=[anywhere, anywhere, anywhere, pl.BlockSpec(memory_space=pltpu.VMEM)],
        out_specs=anywhere,
        scratch_shapes=[
            pltpu.VMEM((SUBSTEPS + 1, fields, half, slab + 2 * HALO), F32),
            pltpu.VMEM((SUBSTEPS, half, slab), F32),
            pltpu.VMEM((SUBSTEPS, half, slab), F32),
            pltpu.VMEM((SUBSTEPS, half, slab), F32),
            pltpu.VMEM((SUBSTEPS, blocks, 1, BLOCK), F32),
            pltpu.VMEM((SUBSTEPS, blocks, 1, BLOCK), F32),
            pltpu.VMEM((blocks, 4, BLOCK + 2 * HALO, BLOCK), BF16),
            pltpu.VMEM((NB, slab), jnp.int32),
            pltpu.VMEM((2, NB, slab), F32),
            pltpu.VMEM((half + 8, 2 * half), BF16),
            pltpu.VMEM((half + 8, 2 * half), BF16),
            dma((2,)),
            dma((blocks, NY - 1)),
            dma((blocks, NY - 1)),
            dma((blocks,)),
            dma((2, blocks, NY - 1)),
            dma((2, blocks, NY - 1)),
            dma((2, blocks)),
            dma((SUBSTEPS, blocks)),
            dma((SUBSTEPS, blocks)),
            dma((SUBSTEPS, blocks)),
            dma((SUBSTEPS, blocks)),
            dma((SUBSTEPS, 2)),
            dma((SUBSTEPS, 2)),
        ],
        compiler_params=pltpu.CompilerParams(
            collective_id=0, has_side_effects=True, vmem_limit_bytes=48 << 20
        ),
    )(prognostic, neighbours, metric, inverses)


def solution(mesh):
    in_specs = (
        P(None, "lev", "tile"),
        P(None, "tile"),
        P(None, None, "tile"),
        P("tile", None, None),
    )
    return jax.shard_map(
        per_device, mesh=mesh, in_specs=in_specs, out_specs=P(None, "lev", "tile"), check_vma=False
    )
```

profile of v0, /device:TPU:80, one launch (start us, length us, event | category | flops | bytes accessed | tf_op | source)
XLA Modules:
  0.0 119.8 jit_solution(11825886668441656324)
XLA Ops:
  0.0 0.0 copy-start
  0.0 1.6 %copy-done = f32[4,16,8192]{2,1,0:T(8,128)S(1)} copy-done((f32[4,16,8192]{2,1,0:T(8,128)S(1)}, f32[4,16,8192]{2,1,0:T(8,128)}, u32[]{:S(2)}) %copy-start) | copy-done | bytes 2097176
  1.6 0.0 copy-start.1
  1.6 0.9 copy-done.1
  2.5 0.0 copy-start.2
  2.5 0.9 copy-done.2
  3.4 0.0 copy-start.3
  3.4 0.8 copy-done.3
  4.3 114.1 %acoustic.1 = f32[4,16,8192]{2,1,0:T(8,128)S(1)} custom-call(f32[4,16,8192]{2,1,0:T(8,128)S(1)} %copy-done, s32[4,8192]{1,0:T(4,128)S(1)} %copy-done.2, f32[2,4,8192]{2,1,0:T(4,128)S(1)} %copy-done.1, f32[1,128,128]{2,1,0:T(8,128)S(1)} %copy-done.3), custom_call_target="tpu_custom_call" | custom-call | tf_op jit(solution)/shard_map/acoustic/pallas_call | solution.py:277
  118.4 1.3 %copy.6 = f32[4,16,8192]{2,1,0:T(8,128)} copy(f32[4,16,8192]{2,1,0:T(8,128)S(1)} %acoustic.1) | data formatting | bytes 4194304
Async XLA Ops:
  0.0 1.6 %copy-start = (f32[4,16,8192]{2,1,0:T(8,128)S(1)}, f32[4,16,8192]{2,1,0:T(8,128)}, u32[]{:S(2)}) copy-start(f32[4,16,8192]{2,1,0:T(8,128)} %prog.1) | copy-start | bytes 6291460
  1.6 0.9 copy-start.1
  2.5 0.9 copy-start.2
  3.4 0.8 copy-start.3
where the time goes:
time: 120 us
  Pallas kernels  114 us (95%)
  local copies, waits for them, and re-layouts  5.6 us (5%)
    pallas_call x1, Pallas kernels, per_device(): pl.pallas_call(kernel, name='acoustic', out_shape=jax.ShapeDtypeStruct(pr...  114 us
    unnamed x9, local copies, waits for them, and re-layouts  5.6 us

commit v1 on v0

--- a/solution.py
+++ b/solution.py
@@ -13,6 +13,7 @@
 NY = 4
 BLOCK = 256
 LAG = 4
+AHEAD = 4
 F32, BF16 = jnp.float32, jnp.bfloat16
 C = 0.4 * 0.5
 
@@ -26,8 +27,8 @@
     return jnp.dot(a, b, preferred_element_type=F32)
 
 
-def kernel(prog, nbrs, metr, inv, out, X, PP, RS, RR, PB, PQ, M, NBV, MTV, IH, IL,
-           lsem, yin_s, yin_r, yin_l, out_s, out_r, out_l, z_s, z_r, b_s, b_r, h_s, h_r):
+def kernel(prog, nbrs, metr, inv, out, X, PP, RS, RR, PB, PQ, M, IV, NBV, MTV, IH, IL,
+           lsem, yin_s, yin_r, yin_l, out_s, out_r, out_l, z_s, z_r, b_s, b_r, h_s, h_r, e_s, e_r, e_l):
     lev, tile = lax.axis_index("lev"), lax.axis_index("tile")
     zh, y = lev // NY, lev % NY
     tiles = lax.axis_size("tile")
@@ -36,6 +37,7 @@
     slab = PP.shape[2]
     blocks = slab // BLOCK
     total = SUBSTEPS * blocks
+    cell_count = prog.shape[2]
 
     def at(yy, tt):
         return {"lev": zh * NY + yy, "tile": tt}
@@ -48,8 +50,10 @@
     def remote(src, dst, ssem, rsem, dev):
         return pltpu.make_async_remote_copy(src, dst, ssem, rsem, device_id=dev, device_id_type=pl.DeviceIdType.MESH)
 
-    def order(i):
-        return jnp.where(i % 2 == 0, i // 2, blocks - 1 - i // 2)
+    def order(s, i):
+        one = jnp.where(i < blocks - 2, i + 1, jnp.where(i == blocks - 2, 0, blocks - 1))
+        two = jnp.where(i < blocks - 4, i + 2, jnp.where(i == blocks - 4, 1, jnp.where(i == blocks - 3, blocks - 2, one)))
+        return jnp.where(s == 0, i, jnp.where(s == 1, one, two))
 
     def cells(c):
         return pl.ds(pl.multiple_of(HALO + c * BLOCK, 128), BLOCK)
@@ -65,6 +69,40 @@
             return pltpu.make_async_copy(src, dst, yin_l.at[c])
         return remote(src, dst, yin_s.at[c, d - 1], yin_r.at[c, d - 1], peers[d])
 
+    def edge(side, d, local=False):
+        yy = (y + d) % NY
+        own = pl.multiple_of(y * rows16, 8)
+        if side == 0:
+            first, put = (yy * slab + cell_count - HALO) % cell_count, 0
+            dev = at(yy, (tile + jnp.where(yy == 0, 1, 0)) % tiles)
+        else:
+            first, put = ((yy + 1) * slab) % cell_count, HALO + slab
+            dev = at(yy, (tile + jnp.where(yy == NY - 1, tiles - 1, 0)) % tiles)
+        src = prog.at[pl.ds(0, 3), :, pl.ds(pl.multiple_of(first, 128), HALO)]
+        dst = X.at[0, pl.ds(0, 3), pl.ds(own, rows16), pl.ds(put, HALO)]
+        if local:
+            return pltpu.make_async_copy(src, dst, e_l.at[side])
+        return remote(src, dst, e_s.at[side, d], e_r.at[side, d], dev)
+
+    outer = (0, NY - 1)
+
+    def edge_start(side):
+        for d in range(1, NY):
+            edge(side, d).start()
+        pl.when(y == outer[side])(lambda: edge(side, 0).start())
+        pl.when(y != outer[side])(lambda: edge(side, 0, True).start())
+
+    def edge_wait(side):
+        for d in range(1, NY):
+            edge(side, d).wait_recv()
+        pl.when(y == outer[side])(lambda: edge(side, 0).wait_recv())
+        pl.when(y != outer[side])(lambda: edge(side, 0, True).wait())
+
+    def edge_drain(side):
+        for d in range(1, NY):
+            edge(side, d).wait_send()
+        pl.when(y == outer[side])(lambda: edge(side, 0).wait_send())
+
     def y_in_start(c):
         for d in range(NY):
             y_in(c, d).start()
@@ -99,19 +137,29 @@
     others = peers[1:] + [partner, left, right]
     for dev in others:
         pl.semaphore_signal(barrier, 1, device_id=dev, device_id_type=pl.DeviceIdType.MESH)
+    for side in range(2):
+        @pl.when(y == outer[side])
+        def _():
+            for yy in range(NY):
+                dev = at(yy, (tile + (1 if side else tiles - 1)) % tiles)
+                pl.semaphore_signal(barrier, 1, device_id=dev, device_id_type=pl.DeviceIdType.MESH)
+
     local = (
         pltpu.make_async_copy(nbrs.at[:, pl.ds(pl.multiple_of(y * slab, 128), slab)], NBV, lsem.at[0]),
         pltpu.make_async_copy(metr.at[:, :, pl.ds(pl.multiple_of(y * slab, 128), slab)], MTV, lsem.at[1]),
     )
+    local = local + (pltpu.make_async_copy(inv.at[0], IV, lsem.at[2]),)
     for copy in local:
         copy.start()
-    pl.semaphore_wait(barrier, len(others))
-    for i in range(3):
-        y_in_start(order(i))
+    pl.semaphore_wait(barrier, len(others) + 2)
+    edge_start(0)
+    for c in range(AHEAD):
+        y_in_start(c)
+    edge_start(1)
     for copy in local:
         copy.wait()
 
-    full = inv[0]
+    full = IV[...]
     swapped = jnp.where(zh == 0, full, pltpu.roll(full, half, 1))
     mine = jnp.concatenate([
         jnp.where(zh == 0, swapped[:half], swapped[half:]),
@@ -179,7 +227,7 @@
         X[s + 1, 3, :, cells(c)] = w
 
     def finish(t):
-        s, c = t // blocks, order(t % blocks)
+        s, c = t // blocks, order(t // blocks, t % blocks)
         for copy in z_copies(s, c):
             copy.wait_recv()
         vertical(s, c)
@@ -199,32 +247,34 @@
 
     def begin(t):
         s, i = t // blocks, t % blocks
-        c = order(i)
+        c = order(s, i)
 
         @pl.when(s == 0)
         def _():
-            @pl.when(i + 3 < blocks)
-            def _():
-                y_in_start(order(i + 3))
-
             build(c)
 
             @pl.when(i == 0)
             def _():
+                edge_wait(0)
                 y_in_wait(0)
-                halo(0, 0).start()
-                y_in_wait(blocks - 1)
-                halo(0, 1).start()
-
-            @pl.when(i + 2 < blocks)
+
+            @pl.when(i + 1 < blocks)
             def _():
-                y_in_wait(order(i + 2))
-
-        @pl.when(i == 0)
+                y_in_wait(i + 1)
+
+            @pl.when(i == blocks - 1)
+            def _():
+                edge_wait(1)
+
+            @pl.when(i + AHEAD < blocks)
+            def _():
+                y_in_start(i + AHEAD)
+
+        @pl.when((s > 0) & (c == 0))
         def _():
             halo(s, 1).wait_recv()
 
-        @pl.when(i == 1)
+        @pl.when((s > 0) & (c == blocks - 1))
         def _():
             halo(s, 0).wait_recv()
 
@@ -263,8 +313,9 @@
         return carry
 
     lax.fori_loop(0, blocks, drain, 0)
-    for s in range(SUBSTEPS):
-        for side in range(2):
+    for side in range(2):
+        edge_drain(side)
+        for s in range(1, SUBSTEPS):
             halo(s, side).wait_send()
 
 
@@ -273,12 +324,12 @@
     half, slab = rows16 * NY, cell_count // NY
     blocks = slab // BLOCK
     dma = pltpu.SemaphoreType.DMA
-    anywhere = pl.BlockSpec(memory_space=pl.ANY)
+    anywhere = pl.BlockSpec(memory_space=pltpu.HBM)
     return pl.pallas_call(
         kernel,
         name="acoustic",
         out_shape=jax.ShapeDtypeStruct(prognostic.shape, F32),
-        in_specs=[anywhere, anywhere, anywhere, pl.BlockSpec(memory_space=pltpu.VMEM)],
+        in_specs=[anywhere, anywhere, anywhere, anywhere],
         out_specs=anywhere,
         scratch_shapes=[
             pltpu.VMEM((SUBSTEPS + 1, fields, half, slab + 2 * HALO), F32),
@@ -288,11 +339,12 @@
             pltpu.VMEM((SUBSTEPS, blocks, 1, BLOCK), F32),
             pltpu.VMEM((SUBSTEPS, blocks, 1, BLOCK), F32),
             pltpu.VMEM((blocks, 4, BLOCK + 2 * HALO, BLOCK), BF16),
+            pltpu.VMEM((2 * half, 2 * half), F32),
             pltpu.VMEM((NB, slab), jnp.int32),
             pltpu.VMEM((2, NB, slab), F32),
             pltpu.VMEM((half + 8, 2 * half), BF16),
             pltpu.VMEM((half + 8, 2 * half), BF16),
-            dma((2,)),
+            dma((3,)),
             dma((blocks, NY - 1)),
             dma((blocks, NY - 1)),
             dma((blocks,)),
@@ -305,9 +357,12 @@
             dma((SUBSTEPS, blocks)),
             dma((SUBSTEPS, 2)),
             dma((SUBSTEPS, 2)),
+            dma((2, NY)),
+            dma((2, NY)),
+            dma((2,)),
         ],
         compiler_params=pltpu.CompilerParams(
-            collective_id=0, has_side_effects=True, vmem_limit_bytes=48 << 20
+            collective_id=0, has_side_effects=True, vmem_limit_bytes=62 << 20
         ),
     )(prognostic, neighbours, metric, inverses)
 

time: 120 us -> 105 us (0.88)
  the two profiles are of different devices: /device:TPU:80 before, /device:TPU:16 now
where the time goes in v1:
time: 105 us; the launch traced here: 104 us
  Pallas kernels  101 us (96%)
  local copies, waits for them, and re-layouts  3.06 us (3%)
    pallas_call x1, Pallas kernels, per_device(): pl.pallas_call(kernel, name='acoustic', out_shape=jax.ShapeDtypeStruct(pr...  101 us
    unnamed x1, local copies, waits for them, and re-layouts  3.06 us

profile of v1, /device:TPU:16, one launch (start us, length us, event | category | flops | bytes accessed | tf_op | source)
XLA Modules:
  0.0 104.4 jit_solution(13159029080069106287)
XLA Ops:
  0.0 101.3 %acoustic.1 = f32[4,16,8192]{2,1,0:T(8,128)} custom-call(f32[4,16,8192]{2,1,0:T(8,128)} %prog.1, s32[4,8192]{1,0:T(4,128)} %nbrs.1, f32[2,4,8192]{2,1,0:T(4,128)} %metr.1, f32[1,128,128]{2,1,0:T(8,128)} %inv.1), custom_call_target="tpu_custom_call" | custom-call | tf_op jit(solution)/shard_map/acoustic/pallas_call | solution.py:328
  101.3 3.1 %copy.6 = f32[4,16,8192]{2,1,0:T(8,128)} copy(f32[4,16,8192]{2,1,0:T(8,128)} %acoustic.1) | data formatting | bytes 4194304

commit v2 on v1

--- a/solution.py
+++ b/solution.py
@@ -13,6 +13,7 @@
 NY = 4
 BLOCK = 256
 LAG = 4
+TAIL = 3
 AHEAD = 4
 F32, BF16 = jnp.float32, jnp.bfloat16
 C = 0.4 * 0.5
@@ -61,13 +62,59 @@
     def lanes(c):
         return pl.ds(pl.multiple_of(c * BLOCK, 128), BLOCK)
 
-    def y_in(c, d):
+    def y_in(c, d, last):
         yy = (y + d) % NY
-        src = prog.at[:, :, pl.ds(pl.multiple_of(yy * slab + c * BLOCK, 128), BLOCK)]
-        dst = X.at[0, :, pl.ds(pl.multiple_of(y * rows16, 8), rows16), cells(c)]
-        if d == 0:
-            return pltpu.make_async_copy(src, dst, yin_l.at[c])
-        return remote(src, dst, yin_s.at[c, d - 1], yin_r.at[c, d - 1], peers[d])
+        from_cell, count = c * BLOCK + HALO, BLOCK
+        if last:
+            count = BLOCK - HALO
+        if isinstance(c, int) and c == 0:
+            from_cell, count = 0, BLOCK + HALO
+        parts = (
+            (pl.ds(0, 3), from_cell, count),
+            (pl.ds(3, 1), c * BLOCK, BLOCK),
+        )
+        copies = []
+        for k, (fields, cell, width) in enumerate(parts):
+            src = prog.at[fields, :, pl.ds(pl.multiple_of(yy * slab + cell, 128), width)]
+            dst = X.at[0, fields, pl.ds(pl.multiple_of(y * rows16, 8), rows16), pl.ds(pl.multiple_of(HALO + cell, 128), width)]
+            if d == 0:
+                copies.append(pltpu.make_async_copy(src, dst, yin_l.at[k, c]))
+            else:
+                copies.append(remote(src, dst, yin_s.at[k, c, d - 1], yin_r.at[k, c, d - 1], peers[d]))
+        return copies
+
+    def y_in_each(c, what):
+        if isinstance(c, int):
+            what(c, c == blocks - 1)
+        else:
+            pl.when((c > 0) & (c < blocks - 1))(lambda: what(c, False))
+            pl.when(c == blocks - 1)(lambda: what(blocks - 1, True))
+
+    def y_in_start(c):
+        def start(c, last):
+            for d in range(NY):
+                for copy in y_in(c, d, last):
+                    copy.start()
+
+        y_in_each(c, start)
+
+    def y_in_wait(c):
+        def wait(c, last):
+            for copy in y_in(c, 0, last):
+                copy.wait()
+            for d in range(1, NY):
+                for copy in y_in(c, d, last):
+                    copy.wait_recv()
+
+        y_in_each(c, wait)
+
+    def y_in_sent(c):
+        def sent(c, last):
+            for d in range(1, NY):
+                for copy in y_in(c, d, last):
+                    copy.wait_send()
+
+        y_in_each(c, sent)
 
     def edge(side, d, local=False):
         yy = (y + d) % NY
@@ -103,15 +150,6 @@
             edge(side, d).wait_send()
         pl.when(y == outer[side])(lambda: edge(side, 0).wait_send())
 
-    def y_in_start(c):
-        for d in range(NY):
-            y_in(c, d).start()
-
-    def y_in_wait(c):
-        y_in(c, 0).wait()
-        for d in range(1, NY):
-            y_in(c, d).wait_recv()
-
     def y_out(f, c, d):
         yy = (y + d) % NY
         src = X.at[SUBSTEPS, pl.ds(2 * f, 2), pl.ds(pl.multiple_of(yy * rows16, 8), rows16), cells(c)]
@@ -119,6 +157,10 @@
         if d == 0:
             return pltpu.make_async_copy(src, dst, out_l.at[f, c])
         return remote(src, dst, out_s.at[f, c, d - 1], out_r.at[f, c, d - 1], peers[d])
+
+    def y_out_wait(f, c):
+        for d in range(NY):
+            y_out(f, c, d).wait()
 
     def z_copies(s, c):
         return (
@@ -229,7 +271,7 @@
     def finish(t):
         s, c = t // blocks, order(t // blocks, t % blocks)
         for copy in z_copies(s, c):
-            copy.wait_recv()
+            copy.wait()
         vertical(s, c)
 
         @pl.when((s < SUBSTEPS - 1) & (c == 0))
@@ -244,6 +286,11 @@
         def _():
             for d in range(NY):
                 y_out(1, c, d).start()
+            y_out_wait(0, c)
+
+            @pl.when(t % blocks >= TAIL)
+            def _():
+                y_out_wait(1, order(s, t % blocks - TAIL))
 
     def begin(t):
         s, i = t // blocks, t % blocks
@@ -258,9 +305,7 @@
                 edge_wait(0)
                 y_in_wait(0)
 
-            @pl.when(i + 1 < blocks)
-            def _():
-                y_in_wait(i + 1)
+            y_in_wait(i)
 
             @pl.when(i == blocks - 1)
             def _():
@@ -270,6 +315,11 @@
             def _():
                 y_in_start(i + AHEAD)
 
+        @pl.when(s == 1)
+        def _():
+            pl.when(i == 0)(lambda: y_in_sent(0))
+            y_in_sent(i)
+
         @pl.when((s > 0) & (c == 0))
         def _():
             halo(s, 1).wait_recv()
@@ -296,27 +346,19 @@
         def _():
             begin(t)
 
+        @pl.when(t == total)
+        def _():
+            for side in range(2):
+                edge_drain(side)
+                for s in range(1, SUBSTEPS):
+                    halo(s, side).wait_send()
+
         return carry
 
     lax.fori_loop(0, total + LAG, step, 0)
 
-    def drain(c, carry):
-        for d in range(1, NY):
-            y_in(c, d).wait_send()
-        for f in range(2):
-            y_out(f, c, 0).wait()
-            for d in range(1, NY):
-                y_out(f, c, d).wait()
-        for s in range(SUBSTEPS):
-            for copy in z_copies(s, c):
-                copy.wait_send()
-        return carry
-
-    lax.fori_loop(0, blocks, drain, 0)
-    for side in range(2):
-        edge_drain(side)
-        for s in range(1, SUBSTEPS):
-            halo(s, side).wait_send()
+    for i in range(blocks - TAIL, blocks):
+        y_out_wait(1, order(SUBSTEPS - 1, i))
 
 
 def per_device(prognostic, neighbours, metric, inverses):
@@ -345,9 +387,9 @@
             pltpu.VMEM((half + 8, 2 * half), BF16),
             pltpu.VMEM((half + 8, 2 * half), BF16),
             dma((3,)),
-            dma((blocks, NY - 1)),
-            dma((blocks, NY - 1)),
-            dma((blocks,)),
+            dma((2, blocks, NY - 1)),
+            dma((2, blocks, NY - 1)),
+            dma((2, blocks)),
             dma((2, blocks, NY - 1)),
             dma((2, blocks, NY - 1)),
             dma((2, blocks)),

time: 105 us -> 103 us (0.981)
  Pallas kernels: 101 us -> 99.6 us
    pallas_call x1, Pallas kernels: 101 us -> 99.6 us  [per_device(): pl.pallas_call(kernel, name='acoustic', out_shape=jax.ShapeDtypeStruct(pr...]
where the time goes in v2:
time: 103 us
  Pallas kernels  99.6 us (97%)
  local copies, waits for them, and re-layouts  3.06 us (3%)
    pallas_call x1, Pallas kernels, per_device(): pl.pallas_call(kernel, name='acoustic', out_shape=jax.ShapeDtypeStruct(pr...  99.6 us
    unnamed x1, local copies, waits for them, and re-layouts  3.06 us

profile of v2, /device:TPU:16, one launch (start us, length us, event | category | flops | bytes accessed | tf_op | source)
XLA Modules:
  0.0 102.7 jit_solution(13524445154603365271)
XLA Ops:
  0.0 99.6 %acoustic.1 = f32[4,16,8192]{2,1,0:T(8,128)} custom-call(f32[4,16,8192]{2,1,0:T(8,128)} %prog.1, s32[4,8192]{1,0:T(4,128)} %nbrs.1, f32[2,4,8192]{2,1,0:T(4,128)} %metr.1, f32[1,128,128]{2,1,0:T(8,128)} %inv.1), custom_call_target="tpu_custom_call" | custom-call | tf_op jit(solution)/shard_map/acoustic/pallas_call | solution.py:370
  99.6 3.1 %copy.6 = f32[4,16,8192]{2,1,0:T(8,128)} copy(f32[4,16,8192]{2,1,0:T(8,128)} %acoustic.1) | data formatting | bytes 4194304

commit v3 on v2

--- a/solution.py
+++ b/solution.py
@@ -197,7 +197,6 @@
     edge_start(0)
     for c in range(AHEAD):
         y_in_start(c)
-    edge_start(1)
     for copy in local:
         copy.wait()
 
@@ -314,6 +313,10 @@
             @pl.when(i + AHEAD < blocks)
             def _():
                 y_in_start(i + AHEAD)
+
+            @pl.when(i == 3)
+            def _():
+                edge_start(1)
 
         @pl.when(s == 1)
         def _():

time: 103 us -> 102 us (level)
  no operation moved by 1% of the time
where the time goes in v3:
time: 102 us
  Pallas kernels  98.9 us (97%)
  local copies, waits for them, and re-layouts  3.06 us (3%)
    pallas_call x1, Pallas kernels, per_device(): pl.pallas_call(kernel, name='acoustic', out_shape=jax.ShapeDtypeStruct(pr...  98.9 us
    unnamed x1, local copies, waits for them, and re-layouts  3.06 us

profile of v3, /device:TPU:16, one launch (start us, length us, event | category | flops | bytes accessed | tf_op | source)
XLA Modules:
  0.0 102.0 jit_solution(8698756715783944236)
XLA Ops:
  0.0 98.9 %acoustic.1 = f32[4,16,8192]{2,1,0:T(8,128)} custom-call(f32[4,16,8192]{2,1,0:T(8,128)} %prog.1, s32[4,8192]{1,0:T(4,128)} %nbrs.1, f32[2,4,8192]{2,1,0:T(4,128)} %metr.1, f32[1,128,128]{2,1,0:T(8,128)} %inv.1), custom_call_target="tpu_custom_call" | custom-call | tf_op jit(solution)/shard_map/acoustic/pallas_call | solution.py:373
  99.0 3.1 %copy.6 = f32[4,16,8192]{2,1,0:T(8,128)} copy(f32[4,16,8192]{2,1,0:T(8,128)} %acoustic.1) | data formatting | bytes 4194304

commit v4 on v3

--- a/solution.py
+++ b/solution.py
@@ -194,8 +194,9 @@
     for copy in local:
         copy.start()
     pl.semaphore_wait(barrier, len(others) + 2)
+    y_in_start(0)
     edge_start(0)
-    for c in range(AHEAD):
+    for c in range(1, AHEAD):
         y_in_start(c)
     for copy in local:
         copy.wait()

time: 102 us -> 108 us (1.059)
  the two profiles are of different devices: /device:TPU:16 before, /device:TPU:64 now
where the time goes in v4:
time: 108 us; the launch traced here: 107 us
  Pallas kernels  104 us (96%)
  local copies, waits for them, and re-layouts  3.06 us (3%)
    pallas_call x1, Pallas kernels, per_device(): pl.pallas_call(kernel, name='acoustic', out_shape=jax.ShapeDtypeStruct(pr...  104 us
    unnamed x1, local copies, waits for them, and re-layouts  3.06 us

profile of v4, /device:TPU:64, one launch (start us, length us, event | category | flops | bytes accessed | tf_op | source)
XLA Modules:
  0.0 107.4 jit_solution(12079054783412576127)
XLA Ops:
  0.0 104.4 %acoustic.1 = f32[4,16,8192]{2,1,0:T(8,128)} custom-call(f32[4,16,8192]{2,1,0:T(8,128)} %prog.1, s32[4,8192]{1,0:T(4,128)} %nbrs.1, f32[2,4,8192]{2,1,0:T(4,128)} %metr.1, f32[1,128,128]{2,1,0:T(8,128)} %inv.1), custom_call_target="tpu_custom_call" | custom-call | tf_op jit(solution)/shard_map/acoustic/pallas_call | solution.py:374
  104.4 3.1 %copy.6 = f32[4,16,8192]{2,1,0:T(8,128)} copy(f32[4,16,8192]{2,1,0:T(8,128)} %acoustic.1) | data formatting | bytes 4194304
